TPU v7x, 32 devices: a whole 2x2x4 slice. The times are simulated.
32 devices in a mesh: groups: 2 (over y), ctx: 8 (over z, x), head: 2 (over core).
Axes of the slice: x: 2, y: 2, z: 4, core: 2. Of those that a mesh axis runs over, the one named last changes fastest.
Arguments:
- tokens: bfloat16 [6144, 4096], P(('groups', 'ctx'), 'head'), parts along dimension 0, may hold values from -6 to 6
- w_query: bfloat16 [4096, 2048], P('ctx', 'head'), may hold values from -0.09375 to 0.09375
- w_key: bfloat16 [4096, 2048], P('ctx', 'head'), may hold values from -0.09375 to 0.09375
- w_value: bfloat16 [4096, 2048], P('ctx', 'head'), may hold values from -0.09375 to 0.09375
- w_out: bfloat16 [2048, 4096], P('head'), may hold values from -0.125 to 0.125
Outputs:
- layer_out: bfloat16 [6144, 4096], P(('groups', 'ctx'), 'head'), parts along dimension 0
There are 2 independent parts, one for each index of `groups`. A program takes and returns all parts, laid end to end along the dimension named above; an argument that names none is the same for every part. Nothing has to cross between parts.
All inputs are finite; a program needn't handle non-finite values.
Results may differ from a plain program's by a relative error of at most 0.0067.
Values may be sent and summed in bfloat16 or wider, within the bound.
No kernel may reach another device: no remote copies, remote signals or barrier semaphores. Data moves between devices by JAX's collectives and lax.ppermute only.
A program may use at most 128 MiB of HBM per device.

v0:
```python
import jax
import jax.numpy as jnp
from jax import lax
from jax.sharding import PartitionSpec as P

HDIM = 128


def carried_in(value, axis, join, neutral):
    count, mine = (lax.axis_size(axis), lax.axis_index(axis))
    pieces = lax.all_gather(value, axis)
    total = jnp.full_like(value, 0) + jnp.asarray(neutral, value.dtype)

    def lap(position, total):
        longer = join(total, pieces[position])
        return jnp.where(position < mine, longer, total)

    return lax.fori_loop(0, count - 1, lap, total)


def add_panel(gathered, panel):
    return jnp.dot(gathered, panel, preferred_element_type=jnp.float32)


def combine_sum(earlier_sum, later_sum):
    return earlier_sum + later_sum


def split_heads(matrix):
    return matrix.reshape(matrix.shape[0], matrix.shape[1] // HDIM, HDIM)


def prefix_states(key_rows, value_rows):
    own_state = jnp.einsum("thd,the->hde", key_rows, value_rows, preferred_element_type=jnp.float32)
    return carried_in(own_state, "ctx", combine_sum, jnp.zeros_like(own_state))


def local(tokens, w_query, w_key, w_value, w_out):
    gathered = lax.all_gather(tokens, "head", axis=1, tiled=True)
    row_count = gathered.shape[0]

    def add_one(panel):
        return add_panel(gathered, panel)

    query_sum = add_one(lax.all_gather(w_query, "ctx", axis=0, tiled=True))
    key_sum = add_one(lax.all_gather(w_key, "ctx", axis=0, tiled=True))
    value_sum = add_one(lax.all_gather(w_value, "ctx", axis=0, tiled=True))
    key_rows = split_heads(jax.nn.silu(key_sum).astype(jnp.bfloat16))
    value_rows = split_heads(value_sum.astype(jnp.bfloat16))
    earlier = prefix_states(key_rows, value_rows)
    query_rows = split_heads(jax.nn.silu(query_sum).astype(jnp.bfloat16))
    position = lax.broadcasted_iota(jnp.int32, (row_count, row_count), 0)
    other = lax.broadcasted_iota(jnp.int32, (row_count, row_count), 1)
    causal = other <= position
    scores = jnp.einsum("thd,shd->hts", query_rows, key_rows, preferred_element_type=jnp.float32)
    weights = jnp.where(causal[None], scores, 0.0).astype(jnp.bfloat16)
    mixed = jnp.einsum("hts,she->the", weights, value_rows, preferred_element_type=jnp.float32)
    mixed = mixed + jnp.einsum(
        "thd,hde->the", query_rows, earlier.astype(jnp.bfloat16), preferred_element_type=jnp.float32
    )
    normed = mixed * lax.rsqrt(jnp.mean(mixed * mixed, axis=-1, keepdims=True) + 1e-06)
    normed = normed.astype(jnp.bfloat16).reshape(row_count, -1)
    head_terms = jnp.dot(normed, w_out, preferred_element_type=jnp.float32)
    return lax.psum_scatter(head_terms, "head", scatter_dimension=1, tiled=True).astype(
        jnp.bfloat16
    )


def solution(mesh):
    in_specs = (
        P(("groups", "ctx"), "head"),
        P("ctx", "head"),
        P("ctx", "head"),
        P("ctx", "head"),
        P("head", None),
    )
    out_specs = P(("groups", "ctx"), "head")
    return jax.shard_map(local, mesh=mesh, in_specs=in_specs, out_specs=out_specs, check_vma=False)
```

profile of v0, /device:TPU:0, one launch (start us, length us, event | category | flops | bytes accessed | tf_op | source)
XLA Modules:
  0.0 518.0 jit_solution(9432414339889200614)
XLA Ops:
  6.5 0.7 all-gather.7.cloned.1.call-update
  7.3 0.7 all-gather.13.cloned.1.call-update
  9.4 14.4 %all-gather.7.cloned.1.call-done = bf16[384,4096]{1,0:T(8,128)(2,1)} async-done(((bf16[384,2048]{1,0:T(8,128)(2,1)}), bf16[384,4096]{1,0:T(8,128)(2,1)}) %all-gather.7.cloned.1.call-update) | async-done | bytes 3145744 | tf_op jit(solution)/shard_map/all_gather | solution.py:39
  23.8 128.2 %all-gather.13.cloned.1.call-done = bf16[4096,1024]{1,0:T(8,128)(2,1)} async-done(((bf16[512,1024]{1,0:T(8,128)(2,1)}), bf16[4096,1024]{1,0:T(8,128)(2,1)}) %all-gather.13.cloned.1.call-update) | async-done | bytes 8388624 | tf_op jit(solution)/shard_map/all_gather | solution.py:46
  152.0 7.9 %multiply_convert_fusion = bf16[384,1024]{1,0:T(8,128)(2,1)S(1)} fusion(bf16[384,4096]{1,0:T(8,128)(2,1)} %all-gather.7.cloned.1.call-done, bf16[4096,1024]{1,0:T(8,128)(2,1)} %all-gather.13.cloned.1.call-done), kind=kOutput, calls=%fused_computation.10 | convolution fusion | flops 3223191552 | bytes 12320768 | tf_op jit(solution)/shard_map/dot_general | solution.py:22
  160.3 116.9 %all-gather.9.cloned.1.call-done = bf16[4096,1024]{1,0:T(8,128)(2,1)} async-done(((bf16[512,1024]{1,0:T(8,128)(2,1)}), bf16[4096,1024]{1,0:T(8,128)(2,1)}) %all-gather.9.cloned.1.call-update) | async-done | bytes 8388624 | tf_op jit(solution)/shard_map/all_gather | solution.py:47
  277.2 7.7 %fusion.7 = bf16[48,8,8,128]{3,2,1,0:T(8,128)(2,1)S(1)} fusion(bf16[384,4096]{1,0:T(8,128)(2,1)} %all-gather.7.cloned.1.call-done, bf16[4096,1024]{1,0:T(8,128)(2,1)} %all-gather.9.cloned.1.call-done), kind=kOutput, calls=%fused_computation.14 | convolution fusion | flops 3221618688 | bytes 12320768 | tf_op jit(solution)/shard_map/dot_general | solution.py:22
  285.0 0.9 copy-done.1
  285.9 1.2 fusion.12
  287.4 114.9 %all-gather.11.cloned.1.call-done = bf16[4096,1024]{1,0:T(8,128)(2,1)} async-done(((bf16[512,1024]{1,0:T(8,128)(2,1)}), bf16[4096,1024]{1,0:T(8,128)(2,1)}) %all-gather.11.cloned.1.call-update) | async-done | bytes 8388624 | tf_op jit(solution)/shard_map/all_gather | solution.py:45
  402.3 8.8 %fusion.14 = bf16[48,8,8,128]{3,2,1,0:T(8,128)(2,1)} fusion(bf16[384,4096]{1,0:T(8,128)(2,1)} %all-gather.7.cloned.1.call-done, bf16[4096,1024]{1,0:T(8,128)(2,1)} %all-gather.11.cloned.1.call-done), kind=kOutput, calls=%fused_computation.20 | convolution fusion | flops 3223191552 | bytes 12320768 | tf_op jit(solution)/shard_map/dot_general | solution.py:22
  411.1 2.9 fusion
  414.0 61.9 %all-gather.15.cloned.1.call-done = f32[64,128,128]{2,1,0:T(8,128)} async-done(((f32[8,128,128]{2,1,0:T(8,128)}), f32[64,128,128]{2,1,0:T(8,128)}) %all-gather.15.cloned.1.call-update) | async-done | bytes 4194320 | tf_op jit(solution)/shard_map/all_gather | solution.py:11
  475.9 8.8 %while.14 = (s32[]{:T(128)}, f32[8,128,128]{2,1,0:T(8,128)S(1)}, s32[]{:T(128)}, f32[8,8,128,128]{3,2,1,0:T(8,128)}, s32[]{:T(128)}, /*index=5*/s32[]{:T(128)}) while((s32[]{:T(128)}, f32[8,128,128]{2,1,0:T(8,128)S(1)}, s32[]{:T(128)}, f32[8,8,128,128]{3,2,1,0:T(8,128)}, s32[]{:T(128)}, /*index=5*/s32[]{:T(128)}) %tuple.48), condition=%wide.region_1.2_spmd.clone, body=%wide.region_0.1_spmd.clone.sunk | while | flops 393220 | bytes 1572957 | solution.py:18
  475.9 1.3 add_select_fusion.2
  477.2 1.2 add_select_fusion.2
  478.5 1.2 add_select_fusion.2
  479.7 1.2 add_select_fusion.2
  481.0 1.2 add_select_fusion.2
  482.2 1.2 add_select_fusion.2
  483.5 1.2 add_select_fusion.2
  485.4 9.5 %fusion.22 = f32[384,4096]{1,0:T(8,128)} fusion(bf16[384,1024]{0,1:T(8,128)(2,1)S(1)} %bitcast.43, bf16[1024,4096]{1,0:T(8,128)(2,1)} %param.11), kind=kOutput, calls=%fused_computation.29 | convolution fusion | flops 3221225472 | bytes 15466496 | tf_op jit(solution)/shard_map/dot_general | solution.py:63
  495.0 12.9 %reduce-scatter.2.cloned.1.call-done = f32[384,2048]{1,0:T(8,128)} async-done(((f32[384,4096]{1,0:T(8,128)}), f32[384,2048]{1,0:T(8,128)}) %reduce-scatter.2.cloned.1.call-update) | async-done | bytes 3145744 | tf_op jit(solution)/shard_map/reduce_scatter | solution.py:64
  507.9 3.3 convert_element_type.27
  (19 shorter events, 2.7 us)
Async XLA Ops:
  6.5 17.2 %all-gather.7.cloned.1.call-start = ((), (), s32[]{:S(2)}) async-start(), calls=%async_computation.1 | async-start | bytes 4718592 | tf_op jit(solution)/shard_map/all_gather | solution.py:39
  7.3 144.8 %all-gather.13.cloned.1.call-start = ((), (), s32[]{:S(2)}) async-start(), calls=%async_computation.4 | async-start | bytes 9437184 | tf_op jit(solution)/shard_map/all_gather | solution.py:46
  8.0 269.2 %all-gather.9.cloned.1.call-start = ((), (), s32[]{:S(2)}) async-start(), calls=%async_computation.2 | async-start | bytes 9437184 | tf_op jit(solution)/shard_map/all_gather | solution.py:47
  8.7 393.6 %all-gather.11.cloned.1.call-start = ((), (), s32[]{:S(2)}) async-start(), calls=%async_computation.3 | async-start | bytes 9437184 | tf_op jit(solution)/shard_map/all_gather | solution.py:45
  9.3 466.6 %all-gather.15.cloned.1.call-start = ((), (), s32[]{:S(2)}) async-start(), calls=%async_computation.6 | async-start | bytes 4718592 | tf_op jit(solution)/shard_map/all_gather | solution.py:11
  285.0 0.9 copy-start.1
  287.1 220.8 %reduce-scatter.2.cloned.1.call-start = ((), (), s32[]{:S(2)}) async-start(), calls=%async_computation.5 | async-start | bytes 9437184 | tf_op jit(solution)/shard_map/reduce_scatter | solution.py:64
  475.9 8.8 %copy-start = (bf16[48,8,8,128]{3,2,1,0:T(8,128)(2,1)S(1)}, bf16[48,8,8,128]{3,2,1,0:T(8,128)(2,1)}, u32[]{:S(2)}) copy-start(bf16[48,8,8,128]{3,2,1,0:T(8,128)(2,1)} %fusion.14) | copy-start | bytes 2359300
Sparse Core Ops, SparseCore 0:
  8.9 14.8 all-gather.6
  25.9 126.0 all-gather.12
  154.1 123.0 all-gather.8
  279.2 123.0 all-gather.10
  404.3 71.5 all-gather.14
  495.1 12.7 reduce-scatter.1
where the time goes:
time: 519 us; the launch traced here: 518 us
  waiting for transfers between devices  452 us (87%)
  matrix products  38.5 us (7%)
  between operations  13.6 us (3%)
  other arithmetic  12.1 us (2%)
    all_gather x1, waiting for transfers between devices, local(): key_sum = add_one(lax.all_gather(w_key, 'ctx', axis=0, tiled=True))  128 us
    all_gather x1, waiting for transfers between devices, local(): value_sum = add_one(lax.all_gather(w_value, 'ctx', axis=0, tiled=True))  117 us
    all_gather x1, waiting for transfers between devices, local(): query_sum = add_one(lax.all_gather(w_query, 'ctx', axis=0, tiled=True))  115 us
    all_gather x1, waiting for transfers between devices, carried_in(): pieces = lax.all_gather(value, axis)  61.9 us
    dot_general x3, matrix products, add_panel(): return jnp.dot(gathered, panel, preferred_element_type=jnp.float32)  24.4 us
    all_gather x1, waiting for transfers between devices, local(): gathered = lax.all_gather(tokens, 'head', axis=1, tiled=True)  14.4 us
    reduce_scatter x1, waiting for transfers between devices, local(): lax.psum_scatter(head_terms, 'head', scatter_dimension=1, tiled=True)  12.9 us
  transfers between devices with their start and end apart: 6, of which 6 were waited for; matrix products, arithmetic and copies ran while one was open for 6% of the time, Pallas kernels for 0%

commit v1 on v0

--- a/solution.py
+++ b/solution.py
@@ -4,6 +4,27 @@
 from jax.sharding import PartitionSpec as P
 
 HDIM = 128
+
+
+def ring_gather(shard, axis, dim):
+    count, position, extent = (lax.axis_size(axis), lax.axis_index(axis), shard.shape[dim])
+    right = [(i, (i + 1) % count) for i in range(count)]
+    behind = [(i, (i - 1) % count) for i in range(count)]
+    filled = jnp.zeros((*shard.shape[:dim], count * extent, *shard.shape[dim + 1 :]), shard.dtype)
+    filled = lax.dynamic_update_slice_in_dim(filled, shard, position * extent, axis=dim)
+    from_left = from_right = shard
+    half = count // 2
+    for hop in range(1, half + 1):
+        from_left = lax.ppermute(from_left, axis, right)
+        filled = lax.dynamic_update_slice_in_dim(
+            filled, from_left, (position - hop) % count * extent, axis=dim
+        )
+        if hop < count - half:
+            from_right = lax.ppermute(from_right, axis, behind)
+            filled = lax.dynamic_update_slice_in_dim(
+                filled, from_right, (position + hop) % count * extent, axis=dim
+            )
+    return filled
 
 
 def carried_in(value, axis, join, neutral):
@@ -43,7 +64,7 @@
         return add_panel(gathered, panel)
 
     query_sum = add_one(lax.all_gather(w_query, "ctx", axis=0, tiled=True))
-    key_sum = add_one(lax.all_gather(w_key, "ctx", axis=0, tiled=True))
+    key_sum = add_one(ring_gather(w_key, "ctx", 0))
     value_sum = add_one(lax.all_gather(w_value, "ctx", axis=0, tiled=True))
     key_rows = split_heads(jax.nn.silu(key_sum).astype(jnp.bfloat16))
     value_rows = split_heads(value_sum.astype(jnp.bfloat16))

time: 519 us -> 491 us (0.946)
  waiting for transfers between devices: 452 us -> 364 us
  starting transfers between devices: 0.38 us -> 43.1 us
  local copies, waits for them, and re-layouts: 1.3 us -> 18.1 us
    ppermute x0 -> x7, waiting for transfers between devices: none -> 178 us  [the longest x4 178 us: ring_gather(): from_left = lax.ppermute(from_left, axis, right)]
    all_gather x1 -> x0, waiting for transfers between devices: 128 us -> none  [local(): key_sum = add_one(lax.all_gather(w_key, 'ctx', axis=0, tiled=True))]
    all_gather x1, waiting for transfers between devices: 117 us -> 0.02 us  [local(): value_sum = add_one(lax.all_gather(w_value, 'ctx', axis=0, tiled=True))]
    ppermute x0 -> x7, starting transfers between devices: none -> 42.7 us  [the longest x3 32.3 us: ring_gather(): from_right = lax.ppermute(from_right, axis, behind)]
    all_gather x1, waiting for transfers between devices: 14.4 us -> 0.01 us  [local(): gathered = lax.all_gather(tokens, 'head', axis=1, tiled=True)]
    dynamic_update_slice x0 -> x8, local copies, waits for them, and re-layouts: none -> 13.3 us  [the longest x4 6.72 us: ring_gather(): lax.dynamic_update_slice_in_dim(filled, from_left, (position - hop) % cou...]
    all_gather x1, waiting for transfers between devices: 115 us -> 109 us  [local(): query_sum = add_one(lax.all_gather(w_query, 'ctx', axis=0, tiled=True))]
  transfers between devices with their start and end apart: 6 -> 12, of which waited for: 6 -> 7; matrix products, arithmetic and copies ran while one was open for 6% -> 10% of each run, Pallas kernels for 0% -> 0%
where the time goes in v1:
time: 491 us; the launch traced here: 490 us
  waiting for transfers between devices  364 us (74%)
  starting transfers between devices  43.1 us (9%)
  matrix products  39.6 us (8%)
  local copies, waits for them, and re-layouts  18.1 us (4%)
  between operations  13.3 us (3%)
  other arithmetic  12.1 us (2%)
    ppermute x4, waiting for transfers between devices, ring_gather(): from_left = lax.ppermute(from_left, axis, right)  178 us
    all_gather x1, waiting for transfers between devices, local(): query_sum = add_one(lax.all_gather(w_query, 'ctx', axis=0, tiled=True))  109 us
    all_gather x1, waiting for transfers between devices, carried_in(): pieces = lax.all_gather(value, axis)  61.9 us
    ppermute x3, starting transfers between devices, ring_gather(): from_right = lax.ppermute(from_right, axis, behind)  32.3 us
    dot_general x3, matrix products, add_panel(): return jnp.dot(gathered, panel, preferred_element_type=jnp.float32)  25.5 us
    reduce_scatter x1, waiting for transfers between devices, local(): lax.psum_scatter(head_terms, 'head', scatter_dimension=1, tiled=True)  12.9 us
    ppermute x4, starting transfers between devices, ring_gather(): from_left = lax.ppermute(from_left, axis, right)  10.4 us
  transfers between devices with their start and end apart: 12, of which 7 were waited for; matrix products, arithmetic and copies ran while one was open for 10% of the time, Pallas kernels for 0%

profile of v1, /device:TPU:0, one launch (start us, length us, event | category | flops | bytes accessed | tf_op | source)
XLA Modules:
  0.0 490.1 jit_solution(11367794651571865066)
XLA Ops:
  8.8 3.0 collective-permute-start
  11.8 3.1 collective-permute-start.1
  14.9 53.3 %collective-permute-done = bf16[512,1024]{1,0:T(8,128)(2,1)S(1)} collective-permute-done((bf16[512,1024]{1,0:T(8,128)(2,1)}, bf16[512,1024]{1,0:T(8,128)(2,1)S(1)}, u32[]{:S(2)}, u32[]{:S(2)}) %collective-permute-start) | collective-permute-done | bytes 1048608 | tf_op jit(solution)/shard_map/ppermute | solution.py:18
  68.2 2.4 collective-permute-start.2
  70.6 3.0 collective-permute-start.3
  73.6 59.5 %collective-permute-done.2 = bf16[512,1024]{1,0:T(8,128)(2,1)S(1)} collective-permute-done((bf16[512,1024]{1,0:T(8,128)(2,1)S(1)}, bf16[512,1024]{1,0:T(8,128)(2,1)S(1)}, u32[]{:S(2)}, u32[]{:S(2)}) %collective-permute-start.2) | collective-permute-done | bytes 1048608 | tf_op jit(solution)/shard_map/ppermute | solution.py:18
  133.1 2.5 collective-permute-start.4
  135.6 26.1 %collective-permute-start.5 = (bf16[512,1024]{1,0:T(8,128)(2,1)}, bf16[512,1024]{1,0:T(8,128)(2,1)}, u32[]{:S(2)}, u32[]{:S(2)}) collective-permute-start(bf16[512,1024]{1,0:T(8,128)(2,1)} %collective-permute-done.3), channel_id=1, source_target_pairs={{0,14},{2,0},{4,2},{6,4},{8,6},{10,8},{12,10},{14,12},{1,15},{3,1}... | collective-permute-start | bytes 3145736 | tf_op jit(solution)/shard_map/ppermute | solution.py:23
  161.8 40.2 %collective-permute-done.4 = bf16[512,1024]{1,0:T(8,128)(2,1)} collective-permute-done((bf16[512,1024]{1,0:T(8,128)(2,1)S(1)}, bf16[512,1024]{1,0:T(8,128)(2,1)}, u32[]{:S(2)}, u32[]{:S(2)}) %collective-permute-start.4) | collective-permute-done | bytes 1048608 | tf_op jit(solution)/shard_map/ppermute | solution.py:18
  201.9 2.6 collective-permute-start.6
  204.5 4.3 broadcast_in_dim.21
  213.1 2.3 constant_dynamic-update-slice_fusion.3
  219.9 24.8 %collective-permute-done.6 = bf16[512,1024]{1,0:T(8,128)(2,1)} collective-permute-done((bf16[512,1024]{1,0:T(8,128)(2,1)}, bf16[512,1024]{1,0:T(8,128)(2,1)}, u32[]{:S(2)}, u32[]{:S(2)}) %collective-permute-start.6) | collective-permute-done | bytes 1048608 | tf_op jit(solution)/shard_map/ppermute | solution.py:18
  244.8 2.3 constant_dynamic-update-slice_fusion
  247.1 7.9 %fusion.10 = bf16[384,1024]{1,0:T(8,128)(2,1)S(1)} fusion(bf16[384,4096]{1,0:T(8,128)(2,1)} %all-gather.6.cloned.1.call-done, bf16[4096,1024]{1,0:T(8,128)(2,1)} %constant_dynamic-update-slice_fusion), kind=kOutput, calls=%fused_computation.16 | convolution fusion | flops 3223191552 | bytes 12320768 | tf_op jit(solution)/shard_map/dot_general | solution.py:43
  255.4 8.8 %fusion.11 = bf16[48,8,8,128]{3,2,1,0:T(8,128)(2,1)S(1)} fusion(bf16[384,4096]{1,0:T(8,128)(2,1)} %all-gather.6.cloned.1.call-done, bf16[4096,1024]{1,0:T(8,128)(2,1)} %all-gather.8.cloned.1.call-done), kind=kOutput, calls=%fused_computation.19 | convolution fusion | flops 3221618688 | bytes 12320768 | tf_op jit(solution)/shard_map/dot_general | solution.py:43
  265.6 109.2 %all-gather.10.cloned.1.call-done = bf16[4096,1024]{1,0:T(8,128)(2,1)} async-done(((bf16[512,1024]{1,0:T(8,128)(2,1)}), bf16[4096,1024]{1,0:T(8,128)(2,1)}) %all-gather.10.cloned.1.call-update) | async-done | bytes 8388624 | tf_op jit(solution)/shard_map/all_gather | solution.py:66
  374.9 8.8 %fusion.18 = bf16[48,8,8,128]{3,2,1,0:T(8,128)(2,1)} fusion(bf16[384,4096]{1,0:T(8,128)(2,1)} %all-gather.6.cloned.1.call-done, bf16[4096,1024]{1,0:T(8,128)(2,1)} %all-gather.10.cloned.1.call-done), kind=kOutput, calls=%fused_computation.25 | convolution fusion | flops 3223191552 | bytes 12320768 | tf_op jit(solution)/shard_map/dot_general | solution.py:43
  383.6 2.9 fusion
  386.6 61.9 %all-gather.12.cloned.1.call-done = f32[64,128,128]{2,1,0:T(8,128)} async-done(((f32[8,128,128]{2,1,0:T(8,128)}), f32[64,128,128]{2,1,0:T(8,128)}) %all-gather.12.cloned.1.call-update) | async-done | bytes 4194320 | tf_op jit(solution)/shard_map/all_gather | solution.py:32
  448.4 8.7 %while.14 = (s32[]{:T(128)}, f32[8,128,128]{2,1,0:T(8,128)S(1)}, s32[]{:T(128)}, f32[8,8,128,128]{3,2,1,0:T(8,128)}, s32[]{:T(128)}, /*index=5*/s32[]{:T(128)}) while((s32[]{:T(128)}, f32[8,128,128]{2,1,0:T(8,128)S(1)}, s32[]{:T(128)}, f32[8,8,128,128]{3,2,1,0:T(8,128)}, s32[]{:T(128)}, /*index=5*/s32[]{:T(128)}) %tuple.46), condition=%wide.region_1.2_spmd.clone, body=%wide.region_0.1_spmd.clone.sunk | while | flops 393220 | bytes 1572957 | solution.py:39
  457.9 9.5 %fusion.26 = f32[384,4096]{1,0:T(8,128)} fusion(bf16[384,1024]{0,1:T(8,128)(2,1)S(1)} %bitcast.56, bf16[1024,4096]{1,0:T(8,128)(2,1)} %param.11), kind=kOutput, calls=%fused_computation.42 | convolution fusion | flops 3221225472 | bytes 15466496 | tf_op jit(solution)/shard_map/dot_general | solution.py:84
  467.4 12.9 %reduce-scatter.2.cloned.1.call-done = f32[384,2048]{1,0:T(8,128)} async-done(((f32[384,4096]{1,0:T(8,128)}), f32[384,2048]{1,0:T(8,128)}) %reduce-scatter.2.cloned.1.call-update) | async-done | bytes 3145744 | tf_op jit(solution)/shard_map/reduce_scatter | solution.py:85
  480.3 3.3 convert_element_type.27
  (45 shorter events, 22.1 us)
Async XLA Ops:
  6.5 240.5 %all-gather.6.cloned.1.call-start = ((), (), s32[]{:S(2)}) async-start(), calls=%async_computation.1 | async-start | bytes 4718592 | tf_op jit(solution)/shard_map/all_gather | solution.py:60
  7.3 248.1 %all-gather.8.cloned.1.call-start = ((), (), s32[]{:S(2)}) async-start(), calls=%async_computation.2 | async-start | bytes 9437184 | tf_op jit(solution)/shard_map/all_gather | solution.py:68
  8.0 200.9 %copy-start = (bf16[512,1024]{1,0:T(8,128)(2,1)S(1)}, bf16[512,1024]{1,0:T(8,128)(2,1)}, u32[]{:S(2)}) copy-start(bf16[512,1024]{1,0:T(8,128)(2,1)} %param.9) | copy-start | bytes 3145732
  8.0 366.8 %all-gather.10.cloned.1.call-start = ((), (), s32[]{:S(2)}) async-start(), calls=%async_computation.3 | async-start | bytes 9437184 | tf_op jit(solution)/shard_map/all_gather | solution.py:66
  8.8 439.7 %all-gather.12.cloned.1.call-start = ((), (), s32[]{:S(2)}) async-start(), calls=%async_computation.5 | async-start | bytes 4718592 | tf_op jit(solution)/shard_map/all_gather | solution.py:32
  8.8 59.4 %collective-permute-start = (bf16[512,1024]{1,0:T(8,128)(2,1)}, bf16[512,1024]{1,0:T(8,128)(2,1)S(1)}, u32[]{:S(2)}, u32[]{:S(2)}) collective-permute-start(bf16[512,1024]{1,0:T(8,128)(2,1)} %param.9), channel_id=1, source_target_pairs={{0,2},{2,4},{4,6},{6,8},{8,10},{10,12},{12,14},{14,0},{1,3},{3,5},... | collective-permute-start | bytes 3145736 | tf_op jit(solution)/shard_map/ppermute | solution.py:18
  11.8 58.8 %collective-permute-start.1 = (bf16[512,1024]{1,0:T(8,128)(2,1)}, bf16[512,1024]{1,0:T(8,128)(2,1)S(1)}, u32[]{:S(2)}, u32[]{:S(2)}) collective-permute-start(bf16[512,1024]{1,0:T(8,128)(2,1)} %param.9), channel_id=1, source_target_pairs={{0,14},{2,0},{4,2},{6,4},{8,6},{10,8},{12,10},{14,12},{1,15},{3,1}... | collective-permute-start | bytes 3145736 | tf_op jit(solution)/shard_map/ppermute | solution.py:23
  68.2 64.9 %collective-permute-start.2 = (bf16[512,1024]{1,0:T(8,128)(2,1)S(1)}, bf16[512,1024]{1,0:T(8,128)(2,1)S(1)}, u32[]{:S(2)}, u32[]{:S(2)}) collective-permute-start(bf16[512,1024]{1,0:T(8,128)(2,1)S(1)} %collective-permute-done), channel_id=1, source_target_pairs={{0,2},{2,4},{4,6},{6,8},{8,10},{10,12},{12,14},{14,0},{1,3},{3,5},... | collective-permute-start | bytes 3145736 | tf_op jit(solution)/shard_map/ppermute | solution.py:18
  70.6 65.0 %collective-permute-start.3 = (bf16[512,1024]{1,0:T(8,128)(2,1)S(1)}, bf16[512,1024]{1,0:T(8,128)(2,1)}, u32[]{:S(2)}, u32[]{:S(2)}) collective-permute-start(bf16[512,1024]{1,0:T(8,128)(2,1)S(1)} %collective-permute-done.1), channel_id=1, source_target_pairs={{0,14},{2,0},{4,2},{6,4},{8,6},{10,8},{12,10},{14,12},{1,15},{3,1}... | collective-permute-start | bytes 3145736 | tf_op jit(solution)/shard_map/ppermute | solution.py:23
  133.1 2.5 copy-start.1
  133.1 68.8 %collective-permute-start.4 = (bf16[512,1024]{1,0:T(8,128)(2,1)S(1)}, bf16[512,1024]{1,0:T(8,128)(2,1)}, u32[]{:S(2)}, u32[]{:S(2)}) collective-permute-start(bf16[512,1024]{1,0:T(8,128)(2,1)S(1)} %collective-permute-done.2), channel_id=1, source_target_pairs={{0,2},{2,4},{4,6},{6,8},{8,10},{10,12},{12,14},{14,0},{1,3},{3,5},... | collective-permute-start | bytes 3145736 | tf_op jit(solution)/shard_map/ppermute | solution.py:18
  135.6 82.1 %collective-permute-start.5 = (bf16[512,1024]{1,0:T(8,128)(2,1)}, bf16[512,1024]{1,0:T(8,128)(2,1)}, u32[]{:S(2)}, u32[]{:S(2)}) collective-permute-start(bf16[512,1024]{1,0:T(8,128)(2,1)} %collective-permute-done.3), channel_id=1, source_target_pairs={{0,14},{2,0},{4,2},{6,4},{8,6},{10,8},{12,10},{14,12},{1,15},{3,1}... | collective-permute-start | bytes 3145736 | tf_op jit(solution)/shard_map/ppermute | solution.py:23
  201.9 42.8 %collective-permute-start.6 = (bf16[512,1024]{1,0:T(8,128)(2,1)}, bf16[512,1024]{1,0:T(8,128)(2,1)}, u32[]{:S(2)}, u32[]{:S(2)}) collective-permute-start(bf16[512,1024]{1,0:T(8,128)(2,1)} %collective-permute-done.4), channel_id=1, source_target_pairs={{0,2},{2,4},{4,6},{6,8},{8,10},{10,12},{12,14},{14,0},{1,3},{3,5},... | collective-permute-start | bytes 3145736 | tf_op jit(solution)/shard_map/ppermute | solution.py:18
  208.9 3.2 copy-start.2
  264.1 1.2 copy-start.4
  265.4 215.0 %reduce-scatter.2.cloned.1.call-start = ((), (), s32[]{:S(2)}) async-start(), calls=%async_computation.4 | async-start | bytes 9437184 | tf_op jit(solution)/shard_map/reduce_scatter | solution.py:85
  386.6 70.6 %copy-start.3 = (bf16[48,8,8,128]{3,2,1,0:T(8,128)(2,1)S(1)}, bf16[48,8,8,128]{3,2,1,0:T(8,128)(2,1)}, u32[]{:S(2)}) copy-start(bf16[48,8,8,128]{3,2,1,0:T(8,128)(2,1)} %fusion.18) | copy-start | bytes 2359300
Sparse Core Ops, SparseCore 0:
  8.9 14.8 all-gather.5
  25.9 223.9 all-gather.7
  252.0 122.8 all-gather.9
  376.8 71.5 all-gather.11
  467.5 12.7 reduce-scatter.1
